TPU v7x, 128 devices: a whole 4x4x4 slice. The times are simulated.
128 devices in a mesh: dp: 64 (over x, z_hi, y, core), tensor: 2 (over z_lo).
Axes of the slice: x: 4, y: 4, z: 4 (z_hi: 2, z_lo: 2; z = z_hi * 2 + z_lo), core: 2. Of those that a mesh axis runs over, the one named last changes fastest.
Arguments:
- inputs: bfloat16 [16384, 1152], P(('dp', 'tensor')), may hold values from -24 to 24
- doc_ids: int32 [64, 256], P('dp'), may hold values from 0 to 3, never falling along the last dimension, each value on 1 to 128 neighbouring positions
- prenorm: bfloat16 [1152], P('dp'), may hold values from 0.099609375 to 1.8984375
- query_proj: bfloat16 [1152, 1024], P('dp', 'tensor'), may hold values from -0.1875 to 0.1875
- key_proj: bfloat16 [1152, 256], P('dp'), may hold values from -0.1875 to 0.1875
- value_proj: bfloat16 [1152, 256], P('dp'), may hold values from -0.1875 to 0.1875
- querynorm: bfloat16 [256], P('dp'), may hold values from 0.5 to 2
- keynorm: bfloat16 [256], P('dp'), may hold values from 0.5 to 2
- output_proj: bfloat16 [1024, 1152], P('tensor', 'dp'), may hold values from -0.1875 to 0.1875
- postnorm: bfloat16 [1152], P('dp'), may hold values from 0.099609375 to 1.8984375
- ffnnorm: bfloat16 [1152], P('dp'), may hold values from 0.099609375 to 1.8984375
- gate_proj: bfloat16 [1152, 6912], P('dp', 'tensor'), may hold values from -0.1875 to 0.1875
- up_proj: bfloat16 [1152, 6912], P('dp', 'tensor'), may hold values from -0.1875 to 0.1875
- down_proj: bfloat16 [6912, 1152], P('tensor', 'dp'), may hold values from -0.078125 to 0.078125
- endnorm: bfloat16 [1152], P('dp'), may hold values from 0.099609375 to 1.8984375
- cotangent: bfloat16 [16384, 1152], P(('dp', 'tensor')), may hold values from -24 to 24
Outputs:
- layer_out: bfloat16 [16384, 1152], P(('dp', 'tensor'))
- inputs_grad: float32 [16384, 1152], P(('dp', 'tensor'))
- prenorm_grad: float32 [1152], P('dp')
- query_grad: float32 [1152, 1024], P('dp', 'tensor')
- key_grad: float32 [1152, 256], P('dp')
- value_grad: float32 [1152, 256], P('dp')
- querynorm_grad: float32 [256], P('dp')
- keynorm_grad: float32 [256], P('dp')
- output_grad: float32 [1024, 1152], P('tensor', 'dp')
- postnorm_grad: float32 [1152], P('dp')
- ffnnorm_grad: float32 [1152], P('dp')
- gate_grad: float32 [1152, 6912], P('dp', 'tensor')
- up_grad: float32 [1152, 6912], P('dp', 'tensor')
- down_grad: float32 [6912, 1152], P('tensor', 'dp')
- endnorm_grad: float32 [1152], P('dp')
Inputs may be any that keep to these rules, and one draw needn't show every extreme that they name: `doc_ids`: in each sequence the document numbers never fall; every one of the 4 documents has 1 to half of 256 tokens, and some document has exactly half of 256 tokens.
All inputs are finite; a program needn't handle non-finite values.
Results may differ from a plain program's by a relative error of at most 0.025.
Values may be sent and summed in bfloat16 or wider, within the bound.
No kernel may reach another device: no remote copies, remote signals or barrier semaphores. Data moves between devices by JAX's collectives and lax.ppermute only.
A program may use at most 256 MiB of HBM per device.

v0:
```python
from functools import partial
import math

import jax
import jax.numpy as jnp
from jax import lax
from jax.sharding import PartitionSpec as P

H = 4
HD = 256


epsilon = 1e-06
rope_base = 1000000.0
query_scale = 0.0625


def sent_together(arrays, axis, dim, along):
    both = jnp.concatenate(arrays, axis=along)
    whole, at, gathered = (lax.all_gather(both, axis, axis=dim, tiled=True), 0, [])
    for a in arrays:
        gathered.append(lax.slice_in_dim(whole, at, at + a.shape[along], axis=along))
        at += a.shape[along]
    return tuple(gathered)


def gather_turned(arrays, axis, dims):
    turned = [jnp.moveaxis(a, dim, 0) for a, dim in zip(arrays, dims)]
    widths = [t[0].size for t in turned]
    both = jnp.concatenate([t.reshape(-1, w) for t, w in zip(turned, widths)], axis=1)
    whole = lax.all_gather(both, axis, axis=0, tiled=True)
    tiles = jnp.split(whole, [sum(widths[:k]) for k in range(1, len(widths))], axis=1)
    return tuple(
        (
            jnp.moveaxis(b.reshape(-1, *t.shape[1:]), 0, dim)
            for b, t, dim in zip(tiles, turned, dims)
        )
    )


def rms_scale(values, scales):
    mean_sq = jnp.mean(values * values, axis=-1, keepdims=True)
    return values * lax.rsqrt(mean_sq + epsilon) * scales


def head_piece(cos_tab, sin_tab, factor, raw_heads, scales):
    normed = rms_scale(raw_heads, scales)
    half_width = normed.shape[-1] // 2
    first_half = normed[..., :half_width]
    second = normed[..., half_width:]
    cos_rows = cos_tab[:, None, :]
    sin_rows = sin_tab[:, None, :]
    turned = jnp.concatenate(
        [first_half * cos_rows - second * sin_rows, second * cos_rows + first_half * sin_rows],
        axis=-1,
    )
    return turned * factor


def gelu_mix(gate_in, up_in):
    return jax.nn.gelu(gate_in, approximate=True) * up_in


def matmul(left_op, right_op):
    return jnp.dot(left_op, right_op, preferred_element_type=jnp.float32)


def matmul_nt(left_op, right_op):
    return lax.dot_general(
        left_op, right_op, (((1,), (1,)), ((), ())), preferred_element_type=jnp.float32
    )


def matmul_tn(left_op, right_op):
    return lax.dot_general(
        left_op, right_op, (((0,), (0,)), ((), ())), preferred_element_type=jnp.float32
    )


def rope_tables(segment):
    seq_length = segment.shape[0]
    token_index = jnp.arange(seq_length, dtype=jnp.int32)
    same_doc = segment[:, None] == segment[None, :]
    earlier = token_index[None, :] < token_index[:, None]
    position = jnp.sum(jnp.where(same_doc & earlier, 1, 0).astype(jnp.int32), axis=1).astype(
        jnp.float32
    )
    freq_rates = jnp.exp(jnp.arange(HD // 2, dtype=jnp.float32) * (-2.0 * math.log(rope_base) / HD))
    angles = position[:, None] * freq_rates[None, :]
    allowed = same_doc & (token_index[None, :] <= token_index[:, None])
    return (jnp.cos(angles), jnp.sin(angles), allowed)


def widen_rows(local_rows):
    return lax.all_gather(local_rows, "tensor", axis=0, tiled=True)


def narrow_rows(partial_rows):
    return lax.psum_scatter(partial_rows, "tensor", scatter_dimension=0, tiled=True)


def on_device(
    inputs,
    doc_ids,
    prenorm,
    query_proj,
    key_proj,
    value_proj,
    querynorm,
    keynorm,
    output_proj,
    postnorm,
    ffnnorm,
    gate_proj,
    up_proj,
    down_proj,
    endnorm,
    cotangent,
):
    tensor_size = lax.axis_size("tensor")
    local_heads = H // tensor_size
    seq_length = doc_ids.shape[1]
    kv_share = 1.0 / tensor_size
    width_rows = prenorm.shape[0]
    head_rows = querynorm.shape[0]
    attn_set = (
        *sent_together((query_proj, key_proj, value_proj), "dp", 0, 1),
        lax.all_gather(output_proj, "dp", axis=1, tiled=True),
        lax.all_gather(prenorm, "dp", axis=0, tiled=True),
        lax.all_gather(querynorm, "dp", axis=0, tiled=True),
        lax.all_gather(keynorm, "dp", axis=0, tiled=True),
        lax.all_gather(postnorm, "dp", axis=0, tiled=True),
    )
    ffn_set = ()
    query_all, key_all, value_all, out_all = (attn_set[0], attn_set[1], attn_set[2], attn_set[3])
    pre_gain = attn_set[4].astype(jnp.float32)
    qgain = attn_set[5].astype(jnp.float32)
    kgain = attn_set[6].astype(jnp.float32)
    post_gain = attn_set[7].astype(jnp.float32)
    cos_tab, sin_tab, allowed = rope_tables(doc_ids[0])
    mask_rows = jnp.repeat(allowed, local_heads, axis=0)
    resid = inputs.astype(jnp.float32)
    normed_f, in_back = jax.vjp(rms_scale, resid, pre_gain)
    normed_in = widen_rows(normed_f.astype(jnp.bfloat16))
    q_raw = matmul(normed_in, query_all).reshape(seq_length, local_heads, HD)
    k_raw = matmul(normed_in, key_all).reshape(seq_length, 1, HD)
    values_b = matmul(normed_in, value_all).astype(jnp.bfloat16)
    q_full, q_back = jax.vjp(partial(head_piece, cos_tab, sin_tab, query_scale), q_raw, qgain)
    k_full, k_back = jax.vjp(partial(head_piece, cos_tab, sin_tab, 1.0), k_raw, kgain)
    query_rows = q_full.astype(jnp.bfloat16).reshape(seq_length * local_heads, HD)
    keys_b = k_full[:, 0, :].astype(jnp.bfloat16)
    scores = matmul_nt(query_rows, keys_b)
    exp_scores = jnp.where(mask_rows, jnp.exp(scores), 0.0)
    log_total = jnp.log(jnp.sum(exp_scores, axis=1, keepdims=True))
    probs_b = jnp.where(mask_rows, jnp.exp(scores - log_total), 0.0).astype(jnp.bfloat16)
    mixed_rows = matmul(probs_b, values_b).astype(jnp.bfloat16)
    mixed = mixed_rows.reshape(seq_length, local_heads * HD)
    branch = narrow_rows(matmul(mixed, out_all))
    attn_norm, attn_back = jax.vjp(rms_scale, branch, post_gain)
    hidden = resid + attn_norm
    ffn_set = gather_turned(
        (gate_proj, up_proj, down_proj, ffnnorm, endnorm), "dp", (0, 0, 1, 0, 0)
    )
    gate_all, up_all, down_all = (ffn_set[0], ffn_set[1], ffn_set[2])
    ffn_gain = ffn_set[3].astype(jnp.float32)
    end_gain = ffn_set[4].astype(jnp.float32)
    ff_norm, ff_in_back = jax.vjp(rms_scale, hidden, ffn_gain)
    ff_input = widen_rows(ff_norm.astype(jnp.bfloat16))
    gate_f = matmul(ff_input, gate_all)
    up_f = matmul(ff_input, up_all)
    product, mix_back = jax.vjp(gelu_mix, gate_f, up_f)
    act = product.astype(jnp.bfloat16)
    ff_branch = narrow_rows(matmul(act, down_all))
    end_norm, end_back = jax.vjp(rms_scale, ff_branch, end_gain)
    layer_out = (hidden + end_norm).astype(jnp.bfloat16)
    grad_out = cotangent.astype(jnp.float32)
    d_ff, grad_end = end_back(grad_out)
    d_ff_rows = widen_rows(d_ff.astype(jnp.bfloat16))
    d_act = matmul_nt(d_ff_rows, down_all)
    d_gate, d_up = mix_back(d_act)
    d_gate_b = d_gate.astype(jnp.bfloat16)
    d_up_b = d_up.astype(jnp.bfloat16)
    hidden_cols = d_gate_b.shape[1]
    ff_sums = lax.psum_scatter(
        jnp.concatenate(
            [matmul_tn(ff_input, d_gate_b), matmul_tn(ff_input, d_up_b), matmul_tn(d_ff_rows, act)],
            axis=1,
        ),
        "dp",
        scatter_dimension=0,
        tiled=True,
    )
    sent_gate = ff_sums[:, :hidden_cols]
    sent_up = ff_sums[:, hidden_cols : 2 * hidden_cols]
    sent_down = ff_sums[:, 2 * hidden_cols :].T
    d_ff_input = narrow_rows(matmul_nt(d_gate_b, gate_all) + matmul_nt(d_up_b, up_all))
    d_h_part, grad_ffn = ff_in_back(d_ff_input)
    d_hidden = grad_out + d_h_part
    d_branch, grad_post = attn_back(d_hidden)
    d_branch_rows = widen_rows(d_branch.astype(jnp.bfloat16))
    outw_t = matmul_tn(d_branch_rows, mixed)
    d_mixed = matmul_nt(d_branch_rows, out_all).astype(jnp.bfloat16)
    d_mixed_rows = d_mixed.reshape(seq_length * local_heads, HD)
    delta = jnp.sum(
        d_mixed_rows.astype(jnp.float32) * mixed_rows.astype(jnp.float32), axis=1, keepdims=True
    )
    again = matmul_nt(query_rows, keys_b)
    probs_f = jnp.where(mask_rows, jnp.exp(again - log_total), 0.0)
    d_probs = matmul_nt(d_mixed_rows, values_b)
    d_scores = (probs_f * (d_probs - delta)).astype(jnp.bfloat16)
    d_queries = matmul(d_scores, keys_b).reshape(seq_length, local_heads, HD)
    keys_part = matmul_tn(d_scores, query_rows)
    values_part = matmul_tn(probs_f.astype(jnp.bfloat16), d_mixed_rows)
    d_keys, d_values = (
        lax.psum(keys_part.astype(jnp.bfloat16), "tensor").astype(jnp.float32),
        lax.psum(values_part.astype(jnp.bfloat16), "tensor").astype(jnp.float32),
    )
    d_q_raw, grad_qgain = q_back(d_queries)
    d_k_raw, grad_kgain = k_back(d_keys[:, None, :])
    d_q_b = d_q_raw.reshape(seq_length, local_heads * HD).astype(jnp.bfloat16)
    d_k_b = d_k_raw.reshape(seq_length, HD).astype(jnp.bfloat16)
    d_v_b = d_values.astype(jnp.bfloat16)
    grad_query = matmul_tn(normed_in, d_q_b)
    grad_key = matmul_tn(normed_in, d_k_b)
    grad_value = matmul_tn(normed_in, d_v_b)
    d_normed = matmul_nt(d_q_b, query_all) + kv_share * (
        matmul_nt(d_k_b, key_all) + matmul_nt(d_v_b, value_all)
    )
    d_in_part, grad_pre = in_back(narrow_rows(d_normed))
    inputs_grad = d_hidden + d_in_part
    gain_pre, gain_post, gain_ffn, gain_end, gain_q, gain_k = lax.psum(
        (grad_pre, grad_post, grad_ffn, grad_end, grad_qgain, kv_share * grad_kgain),
        ("dp", "tensor"),
    )
    dp_index = lax.axis_index("dp")
    sent_pre = lax.dynamic_slice_in_dim(gain_pre, dp_index * width_rows, width_rows)
    sent_post = lax.dynamic_slice_in_dim(gain_post, dp_index * width_rows, width_rows)
    sent_ffn = lax.dynamic_slice_in_dim(gain_ffn, dp_index * width_rows, width_rows)
    sent_end = lax.dynamic_slice_in_dim(gain_end, dp_index * width_rows, width_rows)
    sent_qgain = lax.dynamic_slice_in_dim(gain_q, dp_index * head_rows, head_rows)
    sent_kgain = lax.dynamic_slice_in_dim(gain_k, dp_index * head_rows, head_rows)
    query_cols = grad_query.shape[1]
    out_cols = outw_t.shape[1]
    flat_query, flat_key, flat_value, flat_outw = (
        lax.psum_scatter(grad_query.reshape(-1), "dp", scatter_dimension=0, tiled=True),
        lax.psum_scatter(grad_key.reshape(-1), "dp", scatter_dimension=0, tiled=True),
        lax.psum_scatter(grad_value.reshape(-1), "dp", scatter_dimension=0, tiled=True),
        lax.psum_scatter(outw_t.reshape(-1), "dp", scatter_dimension=0, tiled=True),
    )
    sent_query = flat_query.reshape(width_rows, query_cols)
    sent_key = flat_key.reshape(width_rows, HD)
    sent_value = flat_value.reshape(width_rows, HD)
    sent_outw = flat_outw.reshape(width_rows, out_cols).T
    return (
        layer_out,
        inputs_grad,
        sent_pre,
        sent_query,
        sent_key,
        sent_value,
        sent_qgain,
        sent_kgain,
        sent_outw,
        sent_post,
        sent_ffn,
        sent_gate,
        sent_up,
        sent_down,
        sent_end,
    )


def solution(mesh):
    return jax.shard_map(
        on_device,
        mesh=mesh,
        in_specs=(
            P(("dp", "tensor"), None),
            P("dp", None),
            P("dp"),
            P("dp", "tensor"),
            P("dp", None),
            P("dp", None),
            P("dp"),
            P("dp"),
            P("tensor", "dp"),
            P("dp"),
            P("dp"),
            P("dp", "tensor"),
            P("dp", "tensor"),
            P("tensor", "dp"),
            P("dp"),
            P(("dp", "tensor"), None),
        ),
        out_specs=(
            P(("dp", "tensor"), None),
            P(("dp", "tensor"), None),
            P("dp"),
            P("dp", "tensor"),
            P("dp", None),
            P("dp", None),
            P("dp"),
            P("dp"),
            P("tensor", "dp"),
            P("dp"),
            P("dp"),
            P("dp", "tensor"),
            P("dp", "tensor"),
            P("tensor", "dp"),
            P("dp"),
        ),
        check_vma=False,
    )
```

profile of v0, /device:TPU:0, one launch (start us, length us, event | category | flops | bytes accessed | tf_op | source)
XLA Modules:
  0.0 1493.9 jit_solution(17384775213538259779)
XLA Ops:
  16.4 175.6 %all-reduce.15 = (bf16[1152]{0:T(1024)(128)(2,1)S(1)}, bf16[256]{0:T(256)(128)(2,1)S(1)}, bf16[256]{0:T(256)(128)(2,1)S(1)}, bf16[1152]{0:T(1024)(128)(2,1)}) all-reduce(bf16[1152]{0:T(1024)(128)(2,1)S(1)} %dynamic-update-slice, bf16[256]{0:T(256)(128)(2,1)S(1)} %dynamic-update-slice.2, ...), channel_id=1, replica_groups=mesh['dp'=64,'tensor'=2] {'dp'}, use_global_device_ids=true, to_apply=%add.4 | all-reduce | flops 2816 | bytes 11264
  196.8 7.4 all_gather.34
  205.5 3.1 reshape.393
  241.5 16.1 %reduce-scatter.5.cloned.1.call-done = f32[128,1152]{1,0:T(8,128)} async-done(((f32[256,1152]{1,0:T(8,128)}), f32[128,1152]{1,0:T(8,128)}) %reduce-scatter.5.cloned.1.call-update) | async-done | bytes 589840 | tf_op jit(solution)/shard_map/reduce_scatter | solution.py:99
  260.2 156.6 %all-gather.11.cloned.1.call-done = bf16[64,18,10370]{2,1,0:T(8,128)(2,1)} async-done(((bf16[1,18,10370]{2,1,0:T(8,128)(2,1)}), bf16[64,18,10370]{2,1,0:T(8,128)(2,1)}) %all-gather.11.cloned.1.call-update) | async-done | bytes 23892496 | tf_op jit(solution)/shard_map/all_gather | solution.py:31
  416.8 28.7 %reshape.395 = bf16[1152,10370]{1,0:T(8,128)(2,1)} reshape(bf16[64,18,10370]{2,1,0:T(8,128)(2,1)} %all-gather.11.cloned.1.call-done) | data formatting | bytes 47784960
  447.6 10.0 all_gather.41
  457.7 7.9 fusion.10
  465.5 3.8 copy-done
  469.3 6.1 multiply_convert_fusion.1
  475.4 5.1 fusion.2
  480.5 22.0 %reduce-scatter.7.cloned.1.call-done = f32[128,1152]{1,0:T(8,128)} async-done(((f32[256,1152]{1,0:T(8,128)}), f32[128,1152]{1,0:T(8,128)}) %reduce-scatter.7.cloned.1.call-update) | async-done | bytes 589840 | tf_op jit(solution)/shard_map/reduce_scatter | solution.py:99
  507.9 9.4 all_gather.42
  517.4 10.4 fusion.18
  529.9 4.1 fusion.4
  534.0 5.1 fusion.21
  539.4 9.8 fusion.97
  549.2 7.8 fusion.95
  557.0 9.0 fusion.96
  571.6 8.5 all_gather.43
  595.8 29.6 %all-reduce.22.cloned.1.call-done = (bf16[256,1,256]{0,2,1:T(8,128)(2,1)}, bf16[256,256]{1,0:T(8,128)(2,1)}) async-done(((bf16[256,1,256]{0,2,1:T(8,128)(2,1)}, bf16[256,256]{1,0:T(8,128)(2,1)}), (bf16[256,1,256]{0,2,1:T(8,128)(2,1)}, bf16[256,256]{1,0:T(8,128)(2,1)})) %all-reduce.22.cloned.1.call-update) | async-done | bytes 262160 | tf_op jit(solution)/shard_map/psum | solution.py:215
  633.8 32.7 %pad_maximum_fusion = f32[1152,10368]{1,0:T(8,128)} fusion(f32[1152,3456]{1,0:T(8,128)} %fusion.97, f32[1152,3456]{1,0:T(8,128)} %fusion.96, f32[1152,3456]{1,0:T(8,128)} %fusion.95), kind=kLoop, calls=%fused_computation | loop fusion | flops 23887872 | bytes 95551488 | tf_op jit(solution)/shard_map/concatenate | solution.py:185
  679.2 74.6 %all-reduce.13 = (f32[1152]{0:T(1024)S(1)}, f32[256]{0:T(256)S(1)}, f32[256]{0:T(256)S(1)}, f32[1152]{0:T(1024)S(1)}, f32[1152]{0:T(1024)S(1)}, /*index=5*/f32[1152]{0:T(1024)S(1)}) all-reduce(f32[1152]{0:T(1024)S(1)} %get-tuple-element.25, f32[256]{0:T(256)S(1)} %copy-done.51, ...), channel_id=1, replica_groups=mesh['dp'=64,'tensor'=2] {'dp','tensor'}, use_global_device_ids=true, to_apply=%region_22.23 | all-reduce | flops 5120 | bytes 40960 | tf_op jit(solution)/shard_map/psum | solution.py:231
  759.4 719.5 %all-reduce.20.cloned.1.call-done = (f32[589824]{0:T(1024)}, f32[294912]{0:T(1024)}, f32[294912]{0:T(1024)}, f32[589824]{0:T(1024)}, f32[1152,10368]{1,0:T(8,128)}) async-done(((f32[589824]{0:T(1024)}, f32[294912]{0:T(1024)}, f32[294912]{0:T(1024)}, f32[589824]{0:T(1024)}, f32[1152,10368]{1,0:T(8,128)}), (f32[589824]{0:T(1024)}, f32[294912]{0:T(1024)}, f32[294912]{0:T(1024)}, f32[589824]{0:T(1024)}, ...) | async-done | bytes 54853648
  (261 shorter events, 112.8 us)
Async XLA Ops:
  7.2 198.3 %all-gather.9.cloned.1.call-start = ((), (), s32[]{:S(2)}) async-start(), calls=%async_computation.9 | async-start | bytes 1597440 | tf_op jit(solution)/shard_map/all_gather | solution.py:128
  7.9 200.6 %all-gather.7.cloned.1.call-start = ((), (), s32[]{:S(2)}) async-start(), calls=%async_computation.8 | async-start | bytes 3194880 | tf_op jit(solution)/shard_map/all_gather | solution.py:20
  9.4 248.2 %reduce-scatter.5.cloned.1.call-start = ((), (), s32[]{:S(2)}) async-start(), calls=%async_computation.4 | async-start | bytes 1769472 | tf_op jit(solution)/shard_map/reduce_scatter | solution.py:99
  13.0 206.7 %copy-start.40 = (f32[256]{0:T(256)}, f32[256]{0:T(256)S(1)}, u32[]{:S(2)}) copy-start(f32[256]{0:T(256)S(1)} %convert_element_type.128) | copy-start | bytes 3076
  194.5 35.6 %copy-start.19 = (pred[512,256]{1,0:T(32,128)(4,1)}, pred[512,256]{1,0:T(32,128)(4,1)S(1)}, u32[]{:S(2)}) copy-start(pred[512,256]{1,0:T(32,128)(4,1)S(1)} %reshape.361) | copy-start | bytes 393220
  232.9 25.9 %copy-start.6 = (bf16[128,1152]{1,0:T(8,128)(2,1)S(1)}, bf16[128,1152]{1,0:T(8,128)(2,1)}, u32[]{:S(2)}) copy-start(bf16[128,1152]{1,0:T(8,128)(2,1)} %param.16) | copy-start | bytes 884740
  235.8 24.4 %copy-start.14 = (bf16[256,512]{1,0:T(8,128)(2,1)}, bf16[256,512]{1,0:T(8,128)(2,1)S(1)}, u32[]{:S(2)}) copy-start(bf16[256,512]{1,0:T(8,128)(2,1)S(1)} %reshape.363) | copy-start | bytes 786436
  238.9 177.9 %all-gather.11.cloned.1.call-start = ((), (), s32[]{:S(2)}) async-start(), calls=%async_computation.10 | async-start | bytes 32747520 | tf_op jit(solution)/shard_map/all_gather | solution.py:31
  241.4 261.1 %reduce-scatter.7.cloned.1.call-start = ((), (), s32[]{:S(2)}) async-start(), calls=%async_computation.5 | async-start | bytes 1769472 | tf_op jit(solution)/shard_map/reduce_scatter | solution.py:99
  241.5 175.3 %copy-start.30 = (f32[1152]{0:T(1024)}, f32[1152]{0:T(1024)S(1)}, u32[]{:S(2)}) copy-start(f32[1152]{0:T(1024)S(1)} %convert_element_type.135) | copy-start | bytes 13828
  258.8 186.7 %copy-start.43 = (f32[128]{0:T(128)}, f32[128]{0:T(128)S(1)}, u32[]{:S(2)}) copy-start(f32[128]{0:T(128)S(1)} %fusion.82) | copy-start | bytes 1540
  260.2 185.3 %copy-start.52 = (f32[128]{0:T(128)}, f32[128]{0:T(128)S(1)}, u32[]{:S(2)}) copy-start(f32[128]{0:T(128)S(1)} %get-tuple-element.47) | copy-start | bytes 1540
  260.2 187.3 %copy-start.46 = (f32[128]{0:T(128)}, f32[128]{0:T(128)S(1)}, u32[]{:S(2)}) copy-start(f32[128]{0:T(128)S(1)} %fusion.83) | copy-start | bytes 1540
  457.7 91.5 %copy-start.8 = (bf16[256,1152]{1,0:T(8,128)(2,1)}, bf16[256,1152]{1,0:T(8,128)(2,1)S(1)}, u32[]{:S(2)}) copy-start(bf16[256,1152]{1,0:T(8,128)(2,1)S(1)} %all_gather.41) | copy-start | bytes 1769476
  480.5 85.5 %reduce-scatter.9.cloned.1.call-start = ((), (), s32[]{:S(2)}) async-start(), calls=%async_computation.6 | async-start | bytes 1769472 | tf_op jit(solution)/shard_map/reduce_scatter | solution.py:99
  505.6 22.1 %slice-start = ((s8[24182784]{0:T(1024)(128)(4,1)}), s8[4194304]{0:T(1024)(128)(4,1)S(1)}, s32[]{:S(2)}) async-start(s8[24182784]{0:T(1024)(128)(4,1)} %bitcast.94), calls=%async_computation.13 | async-start | bytes 8388608
  539.1 86.3 %all-reduce.22.cloned.1.call-start = ((), (), s32[]{:S(2)}) async-start(), calls=%async_computation.12 | async-start | bytes 524288 | tf_op jit(solution)/shard_map/psum | solution.py:215
  589.7 36.7 %copy-start.41 = (f32[256]{0:T(256)S(1)}, f32[256]{0:T(256)}, u32[]{:S(2)}) copy-start(f32[256]{0:T(256)} %copy-done.40) | copy-start | bytes 3076
  594.2 83.7 %reduce-scatter.11.cloned.1.call-start = ((), (), s32[]{:S(2)}) async-start(), calls=%async_computation.7 | async-start | bytes 1769472 | tf_op jit(solution)/shard_map/reduce_scatter | solution.py:99
  633.5 33.0 %copy-start.3 = (bf16[256,1152]{1,0:T(8,128)(2,1)S(1)}, bf16[256,1152]{1,0:T(8,128)(2,1)}, u32[]{:S(2)}) copy-start(bf16[256,1152]{1,0:T(8,128)(2,1)} %copy-done.2) | copy-start | bytes 1769476
  633.5 33.0 %copy-start.16 = (bf16[256,2,256]{0,2,1:T(8,128)(2,1)S(1)}, bf16[256,2,256]{0,2,1:T(8,128)(2,1)}, u32[]{:S(2)}) copy-start(bf16[256,2,256]{0,2,1:T(8,128)(2,1)} %fusion.44) | copy-start | bytes 786436
  633.5 845.4 %all-reduce.20.cloned.1.call-start = ((), (), s32[]{:S(2)}) async-start(), calls=%async_computation.11 | async-start | bytes 109707264
  675.7 81.6 %copy-start.54 = (f32[128]{0:T(128)S(1)}, f32[128]{0:T(128)}, u32[]{:S(2)}) copy-start(f32[128]{0:T(128)} %copy-done.53) | copy-start | bytes 1540
  675.8 81.6 %copy-start.10 = (f32[128,1152]{1,0:T(8,128)S(1)}, f32[128,1152]{1,0:T(8,128)}, u32[]{:S(2)}) copy-start(f32[128,1152]{1,0:T(8,128)} %copy-done.9) | copy-start | bytes 1769476
  (48 other events, 350.5 us)
Sparse Core Ops, SparseCore 0:
  11.2 69.4 all-gather.8
  84.5 67.4 all-gather.6
  239.0 18.5 reduce-scatter.4
  261.6 155.1 all-gather.10
  480.6 21.8 reduce-scatter.6
  539.2 25.2 reduce-scatter.8
  594.3 31.0 all-reduce.21
  633.6 25.3 reduce-scatter.10
  675.9 802.9 all-reduce.19
where the time goes:
time: 1500 us; the launch traced here: 1490 us
  waiting for transfers between devices  945 us (63%)
  blocking collectives  286 us (19%)
  matrix products  87.8 us (6%)
  local copies, waits for them, and re-layouts  79.7 us (5%)
  other arithmetic  77 us (5%)
  between operations  18.5 us (1%)
    unnamed x10, waiting for transfers between devices  720 us
    unnamed x1, blocking collectives  176 us
    all_gather x1, waiting for transfers between devices, gather_turned(): whole = lax.all_gather(both, axis, axis=0, tiled=True)  157 us
    psum x1, blocking collectives, on_device(): lax.psum((grad_pre, grad_post, grad_ffn, grad_end, grad_qgain, kv_share *...  74.6 us
    unnamed x146, local copies, waits for them, and re-layouts  59 us
    reduce_scatter x4, waiting for transfers between devices, narrow_rows(): lax.psum_scatter(partial_rows, 'tensor', scatter_dimension=0, tiled=True)  38.1 us
    all_gather x4, blocking collectives, widen_rows(): return lax.all_gather(local_rows, 'tensor', axis=0, tiled=True)  35.3 us
    concatenate x1, other arithmetic, on_device(): jnp.concatenate([matmul_tn(ff_input, d_gate_b), matmul_tn(ff_input, d_up_...  32.7 us
  transfers between devices with their start and end apart: 9, of which 5 were waited for; matrix products, arithmetic and copies ran while one was open for 7% of the time, Pallas kernels for 0%

commit v1 on v0

v1 whole, which is shorter than its diff:
```python
from functools import partial
import math

import jax
import jax.numpy as jnp
from jax import lax
from jax.sharding import Mesh, PartitionSpec as P

H = 4
HD = 256

epsilon = 1e-06
rope_base = 1000000.0
query_scale = 0.0625

AXES = ("x", "zh", "y", "core", "t")
SIZES = (4, 2, 4, 2, 2)
DP = ("x", "zh", "y", "core")
PLANE = ("x", "y")
ZRING = ("zh", "t")
QUAD = ("zh", "core")
LANES = 128

bf16 = jnp.bfloat16
f32 = jnp.float32


def rms_scale(values, scales):
    mean_sq = jnp.mean(values * values, axis=-1, keepdims=True)
    return values * lax.rsqrt(mean_sq + epsilon) * scales


def head_piece(cos_tab, sin_tab, factor, raw_heads, scales):
    normed = rms_scale(raw_heads, scales)
    half_width = normed.shape[-1] // 2
    first_half = normed[..., :half_width]
    second = normed[..., half_width:]
    turned = jnp.concatenate(
        [first_half * cos_tab - second * sin_tab, second * cos_tab + first_half * sin_tab],
        axis=-1,
    )
    return turned * factor


def gelu_mix(gate_in, up_in):
    return jax.nn.gelu(gate_in, approximate=True) * up_in


def matmul(left_op, right_op):
    return jnp.dot(left_op, right_op, preferred_element_type=f32)


def matmul_nt(left_op, right_op):
    return lax.dot_general(
        left_op, right_op, (((1,), (1,)), ((), ())), preferred_element_type=f32
    )


def matmul_tn(left_op, right_op):
    return lax.dot_general(
        left_op, right_op, (((0,), (0,)), ((), ())), preferred_element_type=f32
    )


def along_z(x, step):
    return lax.ppermute(x, ZRING, [(i, (i + step) % 4) for i in range(4)])


def swap(x, axis):
    return lax.ppermute(x, axis, [(0, 1), (1, 0)])


def group_gather(rows):
    near = (rows, along_z(rows, 1), along_z(rows, -1), along_z(rows, 2))
    return jnp.concatenate([*near, *(swap(b, "core") for b in near)], axis=0)


def group_scatter(part):
    n = part.shape[0] // 8
    mine, theirs = part[: 4 * n], part[4 * n :]
    both = mine.astype(f32) + swap(theirs.astype(bf16), "core").astype(f32)
    sent = both[n:].astype(bf16)
    back = (along_z(sent[:n], -1), along_z(sent[n : 2 * n], 1), along_z(sent[2 * n :], 2))
    return both[:n] + (back[0].astype(f32) + back[1].astype(f32) + back[2].astype(f32))


def sum_everywhere(x):
    for axis in ("core", "t", "zh"):
        x = x + swap(x, axis)
    for axis in ("y", "x"):
        for bit in (1, 2):
            x = x + lax.ppermute(x, axis, [(i, i ^ bit) for i in range(4)])
    return x


def mine_first(core, own, sib):
    return jnp.where(core == 0, own, sib), jnp.where(core == 0, sib, own)


def on_device(
    inputs,
    doc_ids,
    prenorm,
    query_proj,
    key_proj,
    value_proj,
    querynorm,
    keynorm,
    output_proj,
    postnorm,
    ffnnorm,
    gate_proj,
    up_proj,
    down_proj,
    endnorm,
    cotangent,
):
    core = lax.axis_index("core")
    tee = lax.axis_index("t")
    plane_index = lax.axis_index(PLANE)
    quad_index = lax.axis_index(QUAD)
    rows = prenorm.shape[0]
    head_rows = querynorm.shape[0]
    width = rows * 64
    tokens = inputs.shape[0]
    seq_length = doc_ids.shape[1]
    half_cols = HD // 2

    pos = jnp.arange(width, dtype=jnp.int32)
    p_x, p_y, p_zh, p_in = (
        pos // (16 * rows),
        pos // (4 * rows) % 4,
        pos // (2 * rows) % 2,
        pos % (2 * rows),
    )
    natural = (p_x * 8 + p_zh * 4 + p_y) * (2 * rows) + p_in
    turn = (pos[:, None] == natural[None, :]).astype(bf16)

    gains = jnp.concatenate(
        [prenorm, postnorm, ffnnorm, endnorm, querynorm, keynorm]
    )
    gains = jnp.pad(gains, (0, LANES - gains.shape[0])).reshape(1, LANES)
    gains = lax.all_gather(gains, QUAD, axis=0, tiled=True)
    gains = lax.all_gather(gains.reshape(1, 4, LANES), PLANE, axis=0, tiled=True)
    gains = gains.astype(f32)

    def width_gain(k):
        return gains[:, :, k * rows : (k + 1) * rows].reshape(width)

    def head_gain(k):
        at = 4 * rows + k * head_rows
        part = gains[:, :, at : at + head_rows].reshape(4, 4, 2, 2, head_rows)
        return part.transpose(0, 2, 1, 3, 4).reshape(HD)

    pre_gain, post_gain, ffn_gain, end_gain = (width_gain(k) for k in range(4))
    qgain, kgain = head_gain(0), head_gain(1)

    kv_pair = (
        lax.dynamic_slice_in_dim(key_proj, tee * half_cols, half_cols, axis=1),
        lax.dynamic_slice_in_dim(value_proj, tee * half_cols, half_cols, axis=1),
    )
    out_t = output_proj.T
    halves = [
        jnp.concatenate(
            [query_proj[:, c * HD : (c + 1) * HD], kv_pair[c], out_t[:, c * HD : (c + 1) * HD]],
            axis=1,
        )
        for c in range(2)
    ]
    piece = halves[0].shape[1]
    keep, give = mine_first(core, halves[0], halves[1])
    got = swap(give, "core")
    first, second = mine_first(core, keep, got)
    attn_part = jnp.stack([first, second])
    attn_part = lax.all_gather(attn_part, ZRING, axis=0, tiled=False)
    attn_part = attn_part.reshape(2, 2, 2 * rows, piece).transpose(0, 2, 1, 3)
    attn_part = attn_part.reshape(4 * rows, 2, piece)
    qkv_cols = HD + half_cols
    attn_part = jnp.concatenate(
        [
            attn_part[:, :, :qkv_cols].reshape(4 * rows, 2 * qkv_cols),
            attn_part[:, :, qkv_cols:].reshape(4 * rows, 2 * HD),
        ],
        axis=1,
    )
    attn_own = lax.all_gather(attn_part, PLANE, axis=0, tiled=True)
    qkv_own, out_own = attn_own[:, : 2 * qkv_cols], attn_own[:, 2 * qkv_cols :]
    qkv_all = jnp.concatenate([qkv_own, swap(qkv_own, "core")], axis=1)
    out_all = jnp.concatenate([out_own, swap(out_own, "core")], axis=1)

    ff_cols = gate_proj.shape[1] // 4
    ff_pad = -(-ff_cols // LANES) * LANES

    def quarters(w):
        w = w.reshape(rows, 4, ff_cols).transpose(1, 0, 2)
        return jnp.pad(w, ((0, 0), (0, 0), (0, ff_pad - ff_cols)))

    ff_part = jnp.concatenate(
        [quarters(gate_proj), quarters(up_proj), quarters(down_proj.T)], axis=2
    )
    ff_part = lax.all_to_all(ff_part, QUAD, 0, 0, tiled=True)
    ff_all = lax.all_gather(
        ff_part.reshape(4 * rows, 3 * ff_pad), PLANE, axis=0, tiled=True
    )
    gate_up_all, down_all = ff_all[:, : 2 * ff_pad], ff_all[:, 2 * ff_pad :]

    resid = matmul(inputs, turn)
    grad_out = matmul(cotangent, turn)
    segment = doc_ids[0]
    order = jnp.arange(seq_length, dtype=jnp.int32)
    own_seg = lax.dynamic_slice_in_dim(segment, tee * tokens, tokens)
    own_at = tee * tokens + jnp.arange(tokens, dtype=jnp.int32)
    peer_seg = lax.dynamic_slice_in_dim(segment, (1 - tee) * tokens, tokens)
    peer_at = (1 - tee) * tokens + jnp.arange(tokens, dtype=jnp.int32)
    position = jnp.sum(
        jnp.where(
            (own_seg[:, None] == segment[None, :]) & (order[None, :] < own_at[:, None]), 1, 0
        ).astype(jnp.int32),
        axis=1,
    ).astype(f32)
    rates = jnp.exp(jnp.arange(HD // 2, dtype=f32) * (-2.0 * math.log(rope_base) / HD))
    angles = position[:, None] * rates[None, :]
    cos_tab, sin_tab = jnp.cos(angles), jnp.sin(angles)
    key_seg = jnp.concatenate([own_seg, peer_seg])
    key_at = jnp.concatenate([own_at, peer_at])
    allowed = (own_seg[:, None] == key_seg[None, :]) & (key_at[None, :] <= own_at[:, None])
    mask_rows = jnp.tile(allowed, (H, 1))

    normed_f, in_back = jax.vjp(rms_scale, resid, pre_gain)
    normed_in = normed_f.astype(bf16)
    qkv = matmul(normed_in, qkv_all)
    q_at = [k * qkv_cols for k in range(4)]
    q_raw = jnp.stack([qkv[:, a : a + HD] for a in q_at])
    kv = [
        jnp.concatenate([qkv[:, a + HD : a + qkv_cols] for a in pair], axis=1)
        for pair in (q_at[:2], q_at[2:])
    ]
    k_raw, v_raw = mine_first(core, kv[0], kv[1])
    q_full, q_back = jax.vjp(partial(head_piece, cos_tab, sin_tab, query_scale), q_raw, qgain)
    k_full, k_back = jax.vjp(partial(head_piece, cos_tab, sin_tab, 1.0), k_raw, kgain)
    query_rows = q_full.astype(bf16).reshape(H * tokens, HD)
    kv_own = jnp.concatenate([k_full.astype(bf16), v_raw.astype(bf16)], axis=1)
    kv_both = jnp.concatenate([kv_own, swap(kv_own, "t")], axis=0)
    keys_b, values_b = kv_both[:, :HD], kv_both[:, HD:]
    scores = matmul_nt(query_rows, keys_b)
    exp_scores = jnp.where(mask_rows, jnp.exp(scores), 0.0)
    log_total = jnp.log(jnp.sum(exp_scores, axis=1, keepdims=True))
    probs_f = jnp.where(mask_rows, jnp.exp(scores - log_total), 0.0)
    probs_b = probs_f.astype(bf16)
    mixed_rows = matmul(probs_b, values_b).astype(bf16)

    def side_by_side(head_rows_of):
        return jnp.concatenate(
            [head_rows_of[h * tokens : (h + 1) * tokens] for h in range(H)], axis=1
        )

    def stacked(cols):
        return jnp.concatenate([cols[:, h * HD : (h + 1) * HD] for h in range(H)], axis=0)

    mixed = side_by_side(mixed_rows)
    branch = matmul_nt(mixed, out_all)
    attn_norm, attn_back = jax.vjp(rms_scale, branch, post_gain)
    hidden = resid + attn_norm

    ff_norm, ff_in_back = jax.vjp(rms_scale, hidden, ffn_gain)
    ff_input = group_gather(ff_norm.astype(bf16))
    gate_up = matmul(ff_input, gate_up_all)
    gate_f, up_f = gate_up[:, :ff_pad], gate_up[:, ff_pad:]
    product, mix_back = jax.vjp(gelu_mix, gate_f, up_f)
    act = product.astype(bf16)
    ff_branch = group_scatter(matmul_nt(act, down_all))
    end_norm, end_back = jax.vjp(rms_scale, ff_branch, end_gain)
    layer_out = matmul_nt((hidden + end_norm).astype(bf16), turn).astype(bf16)

    d_ff, grad_end = end_back(grad_out)
    d_ff_rows = group_gather(d_ff.astype(bf16))
    d_act = matmul(d_ff_rows, down_all)
    d_gate, d_up = mix_back(d_act)
    d_gate_up = jnp.concatenate([d_gate.astype(bf16), d_up.astype(bf16)], axis=1)
    ff_grads = jnp.concatenate(
        [matmul_tn(ff_input, d_gate_up).astype(bf16), matmul_tn(d_ff_rows, act).astype(bf16)],
        axis=1,
    )
    ff_sums = lax.psum_scatter(ff_grads, PLANE, scatter_dimension=0, tiled=True)
    ff_sums = lax.all_to_all(ff_sums.reshape(4, rows, 3 * ff_pad), QUAD, 0, 0, tiled=True)

    def joined(k):
        part = ff_sums[:, :, k * ff_pad : k * ff_pad + ff_cols]
        return part.transpose(1, 0, 2).reshape(rows, 4 * ff_cols).astype(f32)

    sent_gate, sent_up, sent_down = joined(0), joined(1), joined(2).T

    d_ff_input = group_scatter(matmul_nt(d_gate_up, gate_up_all))
    d_h_part, grad_ffn = ff_in_back(d_ff_input)
    d_hidden = grad_out + d_h_part

    d_branch, grad_post = attn_back(d_hidden)
    d_branch_b = d_branch.astype(bf16)
    out_grad = matmul_tn(d_branch_b, mixed).astype(bf16)
    d_mixed = matmul(d_branch_b, out_all).astype(bf16)
    d_mixed_rows = stacked(d_mixed)
    delta = jnp.sum(
        d_mixed_rows.astype(f32) * mixed_rows.astype(f32), axis=1, keepdims=True
    )
    d_probs = matmul_nt(d_mixed_rows, values_b)
    d_scores = (probs_f * (d_probs - delta)).astype(bf16)
    d_queries = matmul(d_scores, keys_b).reshape(H, tokens, HD)
    d_kv = jnp.concatenate(
        [matmul_tn(d_scores, query_rows), matmul_tn(probs_b, d_mixed_rows)], axis=1
    )
    d_kv = d_kv[:tokens] + swap(d_kv[tokens:].astype(bf16), "t").astype(f32)
    d_keys, d_values = d_kv[:, :HD], d_kv[:, HD:]
    d_q_raw, grad_qgain = q_back(d_queries)
    d_k_raw, grad_kgain = k_back(d_keys)
    d_own, d_sib = mine_first(core, d_k_raw.astype(bf16), d_values.astype(bf16))
    d_q_b = d_q_raw.astype(bf16)
    d_pieces = []
    for k in range(4):
        d_side = d_own if k < 2 else d_sib
        d_pieces += [d_q_b[k], d_side[:, k % 2 * half_cols : (k % 2 + 1) * half_cols]]
    d_qkv = jnp.concatenate(d_pieces, axis=1)
    qkv_grad = matmul_tn(normed_in, d_qkv).astype(bf16)
    d_normed = matmul_nt(d_qkv, qkv_all)
    d_in_part, grad_pre = in_back(d_normed)
    inputs_grad = jnp.dot(
        d_hidden + d_in_part,
        turn.T.astype(f32),
        precision=lax.Precision.HIGHEST,
        preferred_element_type=f32,
    )

    def summed(grad):
        n = grad.shape[1] // 2
        both = grad[:, :n].astype(f32) + swap(grad[:, n:], "core").astype(f32)
        return lax.psum_scatter(both.astype(bf16), PLANE, scatter_dimension=0, tiled=True)

    def over_ring(part):
        return jnp.sum(
            lax.all_to_all(part, ZRING, 0, 0, tiled=True).astype(f32), axis=0
        ).reshape(2, rows, part.shape[-1])

    def rows_of_mine(part):
        own, theirs = jnp.where(core == 0, part[0], part[1]), jnp.where(
            core == 0, part[1], part[0]
        )
        return mine_first(core, own, swap(theirs, "core"))

    out_sum = summed(out_grad).reshape(2, 2 * rows, 2, HD).transpose(0, 2, 1, 3)
    out_sum = over_ring(out_sum.reshape(4, 2 * rows, HD))
    sent_outw = jnp.concatenate(rows_of_mine(out_sum), axis=1).T

    qkv_sum = summed(qkv_grad).reshape(2, 2 * rows, 2, qkv_cols)
    q_sum = qkv_sum[..., :HD].transpose(0, 2, 1, 3)
    kv_sum = qkv_sum[..., HD:].reshape(2, 1, 2 * rows, HD)
    qkv_sum = jnp.concatenate([q_sum, jnp.broadcast_to(kv_sum, q_sum.shape)], axis=3)
    qkv_sum = over_ring(qkv_sum.reshape(4, 2 * rows, 2 * HD))
    sum_0, sum_1 = rows_of_mine(qkv_sum)
    sent_query = jnp.concatenate([sum_0[:, :HD], sum_1[:, :HD]], axis=1)
    sent_key, sent_value = sum_0[:, HD:], sum_1[:, HD:]

    gain_sums = sum_everywhere(
        jnp.concatenate([grad_pre, grad_post, grad_ffn, grad_end, grad_qgain, grad_kgain])
    )
    own_at_width = (plane_index * 4 + quad_index) * rows
    own_at_head = lax.axis_index(DP) * head_rows
    sent_pre, sent_post, sent_ffn, sent_end = (
        lax.dynamic_slice_in_dim(gain_sums, k * width + own_at_width, rows) for k in range(4)
    )
    sent_qgain, sent_kgain = (
        lax.dynamic_slice_in_dim(gain_sums, 4 * width + k * HD + own_at_head, head_rows)
        for k in range(2)
    )
    return (
        layer_out,
        inputs_grad,
        sent_pre,
        sent_query,
        sent_key,
        sent_value,
        sent_qgain,
        sent_kgain,
        sent_outw,
        sent_post,
        sent_ffn,
        sent_gate,
        sent_up,
        sent_down,
        sent_end,
    )


def solution(mesh):
    parts = Mesh(mesh.devices.reshape(SIZES), AXES)
    every = (*DP, "t")
    return jax.shard_map(
        on_device,
        mesh=parts,
        in_specs=(
            P(every, None),
            P(DP, None),
            P(DP),
            P(DP, "t"),
            P(DP, None),
            P(DP, None),
            P(DP),
            P(DP),
            P("t", DP),
            P(DP),
            P(DP),
            P(DP, "t"),
            P(DP, "t"),
            P("t", DP),
            P(DP),
            P(every, None),
        ),
        out_specs=(
            P(every, None),
            P(every, None),
            P(DP),
            P(DP, "t"),
            P(DP, None),
            P(DP, None),
            P(DP),
            P(DP),
            P("t", DP),
            P(DP),
            P(DP),
            P(DP, "t"),
            P(DP, "t"),
            P("t", DP),
            P(DP),
        ),
        check_vma=False,
    )
```

time: 1500 us -> 533 us (0.36)
  waiting for transfers between devices: 945 us -> 299 us
  blocking collectives: 286 us -> 55.3 us
  other arithmetic: 77 us -> 22.7 us
  local copies, waits for them, and re-layouts: 79.7 us -> 36.3 us
  starting transfers between devices: 0.83 us -> 35.5 us
  matrix products: 87.8 us -> 59.2 us
    unnamed x10 -> x8, waiting for transfers between devices: 720 us -> 151 us
    unnamed x1 -> x0, blocking collectives: 176 us -> none
    all_gather x3 -> x2, waiting for transfers between devices: 157 us -> 34 us  [the longest x1 34 us: on_device(): attn_own = lax.all_gather(attn_part, PLANE, axis=0, tiled=True)]
    ppermute x0 -> x38, waiting for transfers between devices: none -> 93.3 us  [the longest x12 55 us: along_z(): return lax.ppermute(x, ZRING, [(i, (i + step) % 4) for i in range(4)])]
    psum x1 -> x0, blocking collectives: 74.6 us -> none  [on_device(): lax.psum((grad_pre, grad_post, grad_ffn, grad_end, grad_qgain, kv_share *...]
    unnamed x146 -> x228, local copies, waits for them, and re-layouts: 59 us -> 11.1 us
    reduce_scatter x4 -> x0, waiting for transfers between devices: 38.1 us -> none  [narrow_rows(): lax.psum_scatter(partial_rows, 'tensor', scatter_dimension=0, tiled=True)]
    psum x1 -> x0, waiting for transfers between devices: 29.6 us -> none  [on_device(): lax.psum(keys_part.astype(jnp.bfloat16), 'tensor').astype(jnp.float32)]
  transfers between devices with their start and end apart: 9 -> 46, of which waited for: 5 -> 31; matrix products, arithmetic and copies ran while one was open for 7% -> 12% of each run, Pallas kernels for 0% -> 0%
where the time goes in v1:
time: 533 us; the launch traced here: 524 us
  waiting for transfers between devices  299 us (56%)
  matrix products  59.2 us (11%)
  blocking collectives  55.3 us (10%)
  local copies, waits for them, and re-layouts  36.3 us (7%)
  starting transfers between devices  35.5 us (7%)
  other arithmetic  22.7 us (4%)
  between operations  16.2 us (3%)
    unnamed x8, waiting for transfers between devices  151 us
    ppermute x12, waiting for transfers between devices, along_z(): return lax.ppermute(x, ZRING, [(i, (i + step) % 4) for i in range(4)])  55 us
    all_gather x1, waiting for transfers between devices, on_device(): attn_own = lax.all_gather(attn_part, PLANE, axis=0, tiled=True)  34 us
    ppermute x22, waiting for transfers between devices, swap(): return lax.ppermute(x, axis, [(0, 1), (1, 0)])  29 us
    dot_general x8, matrix products, matmul(): return jnp.dot(left_op, right_op, preferred_element_type=f32)  24.5 us
    all_gather x1, blocking collectives, on_device(): lax.all_gather(gains.reshape(1, 4, LANES), PLANE, axis=0, tiled=True)  22.4 us
    dot_general x7, matrix products, matmul_nt(): lax.dot_general(left_op, right_op, (((1,), (1,)), ((), ())), preferred_el...  17 us
    ppermute x12, starting transfers between devices, along_z(): return lax.ppermute(x, ZRING, [(i, (i + step) % 4) for i in range(4)])  14.5 us
  transfers between devices with their start and end apart: 46, of which 31 were waited for; matrix products, arithmetic and copies ran while one was open for 12% of the time, Pallas kernels for 0%

profile of v1, /device:TPU:0, one launch (start us, length us, event | category | flops | bytes accessed | tf_op | source)
XLA Modules:
  0.0 523.9 jit_solution(13515892965969100104)
XLA Ops:
  10.2 13.5 %all-gather.2 = bf16[8,18,640]{2,1,0:T(8,128)(2,1)S(1)} all-gather(bf16[2,18,640]{2,1,0:T(8,128)(2,1)S(1)} %pad_maximum_fusion.22), channel_id=4, replica_groups=mesh['x'=4,'zh'=2,'y'=4,'core'=2,'t'=2] {'zh','t'}, dimensions={0}, use_global_device_ids=true | all-gather | bytes 230400 | tf_op jit(solution)/shard_map/all_gather | solution.py:175
  25.5 12.8 %all_to_all.20 = bf16[4,18,2688]{2,1,0:T(8,128)(2,1)S(1)} all-to-all(bf16[4,18,2688]{2,1,0:T(8,128)(2,1)S(1)} %fusion.55), channel_id=1, replica_groups=mesh['x'=4,'zh'=2,'y'=4,'core'=2,'t'=2] {'zh','core'}, dimensions={0} | all-to-all | bytes 774144 | tf_op jit(solution)/shard_map/all_to_all | solution.py:201
  39.3 34.0 %all-gather.8.cloned.1.call-done = bf16[1152,1280]{1,0:T(8,128)(2,1)} async-done(((bf16[72,1280]{1,0:T(8,128)(2,1)}), bf16[1152,1280]{1,0:T(8,128)(2,1)}) %all-gather.8.cloned.1.call-update) | async-done | bytes 2949136 | tf_op jit(solution)/shard_map/all_gather | solution.py:186
  76.5 6.6 %all-gather.3 = bf16[4,1,128]{2,1,0:T(2,128)(2,1)S(1)} all-gather(bf16[1,1,128]{2,1,0:T(2,128)(2,1)S(1)} %pad_bitcast_fusion), channel_id=2, replica_groups=mesh['x'=4,'zh'=2,'y'=4,'core'=2,'t'=2] {'zh','core'}, dimensions={0}, use_global_device_ids=true | all-gather | bytes 1280 | tf_op jit(solution)/shard_map/all_gather | solution.py:143
  83.1 22.4 %all-gather.4 = bf16[16,4,128]{2,1,0:T(4,128)(2,1)S(1)} all-gather(bf16[1,4,128]{2,1,0:T(4,128)(2,1)S(1)} %bitcast.137), channel_id=3, replica_groups=mesh['x'=4,'zh'=2,'y'=4,'core'=2,'t'=2] {'x','y'}, dimensions={0}, use_global_device_ids=true | all-gather | bytes 17408 | tf_op jit(solution)/shard_map/all_gather | solution.py:144
  130.8 6.3 %collective-permute-done.6 = bf16[128,1152]{0,1:T(8,128)(2,1)S(1)} collective-permute-done((bf16[128,1152]{0,1:T(8,128)(2,1)S(1)}, bf16[128,1152]{0,1:T(8,128)(2,1)S(1)}, u32[]{:S(2)}, u32[]{:S(2)}) %collective-permute-start.6) | collective-permute-done | bytes 294944 | tf_op jit(solution)/shard_map/ppermute | solution.py:66
  137.1 5.0 collective-permute-done.5
  148.2 8.0 %fusion.16 = f32[1024,1792]{1,0:T(8,128)S(1)} fusion(bf16[1024,1152]{0,1:T(8,128)(2,1)} %constant_dynamic-update-slice_fusion, bf16[1152,2688]{1,0:T(8,128)(2,1)} %all-gather.10.cloned.1.call-done), kind=kOutput, calls=%fused_computation.24 | convolution fusion | flops 4227858432 | bytes 13828096 | tf_op jit(solution)/shard_map/dot_general | solution.py:50
  159.3 4.9 fusion.33
  174.7 11.2 %collective-permute-done.12 = bf16[128,1152]{0,1:T(8,128)(2,1)S(1)} collective-permute-done((bf16[128,1152]{0,1:T(8,128)(2,1)}, bf16[128,1152]{0,1:T(8,128)(2,1)S(1)}, u32[]{:S(2)}, u32[]{:S(2)}) %collective-permute-start.12) | collective-permute-done | bytes 294944 | tf_op jit(solution)/shard_map/ppermute | solution.py:66
  197.2 8.7 %collective-permute-done.17 = bf16[128,1152]{0,1:T(8,128)(2,1)S(1)} collective-permute-done((bf16[128,1152]{0,1:T(8,128)(2,1)S(1)}, bf16[128,1152]{0,1:T(8,128)(2,1)S(1)}, u32[]{:S(2)}, u32[]{:S(2)}) %collective-permute-start.17) | collective-permute-done | bytes 294944 | tf_op jit(solution)/shard_map/ppermute | solution.py:66
  213.2 8.1 %fusion.9 = (bf16[1024,896]{1,0:T(8,128)(2,1)S(1)}, bf16[1024,896]{1,0:T(8,128)(2,1)S(1)}) fusion(f32[1024,1792]{1,0:T(8,128)S(1)} %bitcast.111, bf16[1024,1152]{0,1:T(8,128)(2,1)S(1)} %constant_dynamic-update-slice_fusion.8, bf16[1152,2688]{1,0:T(8,128)(2,1)} %all-gather.10.cloned.1.call-done), kind=kOutput, calls=%fused_computation.16 | convolution fusion | flops 2135949312 | bytes 15433728 | tf_op jit(solution)/shard_map/dot_general | solution.py:50
  232.3 7.4 %collective-permute-done.23 = bf16[128,1152]{0,1:T(8,128)(2,1)S(1)} collective-permute-done((bf16[128,1152]{0,1:T(8,128)(2,1)S(1)}, bf16[128,1152]{0,1:T(8,128)(2,1)S(1)}, u32[]{:S(2)}, u32[]{:S(2)}) %collective-permute-start.23) | collective-permute-done | bytes 294944 | tf_op jit(solution)/shard_map/ppermute | solution.py:66
  241.8 5.2 collective-permute-done.24
  255.0 5.2 collective-permute-done.26
  271.6 5.0 convolution_convert_fusion.3
  276.6 6.1 %convolution_convert_fusion = bf16[1152,1792]{1,0:T(8,128)(2,1)S(1)} fusion(bf16[1024,1152]{0,1:T(8,128)(2,1)} %constant_dynamic-update-slice_fusion, bf16[1024,896]{1,0:T(8,128)(2,1)S(1)} %copy-done.95, bf16[1024,896]{1,0:T(8,128)(2,1)S(1)} %copy-done.93), kind=kOutput, calls=%fused_computation | convolution fusion | flops 4237262848 | bytes 10158080 | tf_op jit(solution)/shard_map/dot_general | solution.py:60
  296.1 4.6 collective-permute-done.29
  320.2 15.1 %reduce-scatter.12.cloned.1.call-done = bf16[72,512]{1,0:T(8,128)(2,1)} async-done(((bf16[1152,512]{1,0:T(8,128)(2,1)}), bf16[72,512]{1,0:T(8,128)(2,1)}) %reduce-scatter.12.cloned.1.call-update) | async-done | bytes 73744
  341.8 5.1 all-to-all-done.2
  347.1 64.5 %reduce-scatter.10.cloned.1.call-done = bf16[72,768]{1,0:T(8,128)(2,1)} async-done(((bf16[1152,768]{1,0:T(8,128)(2,1)}), bf16[72,768]{1,0:T(8,128)(2,1)}) %reduce-scatter.10.cloned.1.call-update) | async-done | bytes 110608
  418.0 6.1 %all-to-all-done.1 = bf16[4,36,512]{2,1,0:T(8,128)(2,1)S(1)} async-done(((bf16[4,36,512]{2,1,0:T(8,128)(2,1)}), bf16[4,36,512]{2,1,0:T(8,128)(2,1)S(1)}, u32[]{:S(2)}, u32[]{:S(2)}) %all-to-all-start.1) | async-done | bytes 147488 | tf_op jit(solution)/shard_map/all_to_all | solution.py:339
  426.1 71.4 %reduce-scatter.14.cloned.1.call-done = bf16[72,2688]{1,0:T(8,128)(2,1)} async-done(((bf16[1152,2688]{1,0:T(8,128)(2,1)}), bf16[72,2688]{1,0:T(8,128)(2,1)}) %reduce-scatter.14.cloned.1.call-update) | async-done | bytes 387088
  505.0 9.0 %all-to-all-done.3 = bf16[4,18,2688]{2,1,0:T(8,128)(2,1)S(1)} async-done(((bf16[4,18,2688]{2,1,0:T(8,128)(2,1)}), bf16[4,18,2688]{2,1,0:T(8,128)(2,1)S(1)}, u32[]{:S(2)}, u32[]{:S(2)}) %all-to-all-start.3) | async-done | bytes 387104 | tf_op jit(solution)/shard_map/all_to_all | solution.py:285
  (467 shorter events, 161.4 us)
Async XLA Ops:
  7.2 66.1 %all-gather.8.cloned.1.call-start = ((), (), s32[]{:S(2)}) async-start(), calls=%async_computation.7 | async-start | bytes 3133440 | tf_op jit(solution)/shard_map/all_gather | solution.py:186
  24.8 123.4 %all-gather.10.cloned.1.call-start = ((), (), s32[]{:S(2)}) async-start(), calls=%async_computation.8 | async-start | bytes 6580224 | tf_op jit(solution)/shard_map/all_gather | solution.py:202
  39.2 296.0 %reduce-scatter.12.cloned.1.call-start = ((), (), s32[]{:S(2)}) async-start(), calls=%async_computation.10 | async-start | bytes 1253376
  76.2 32.9 %collective-permute-start.1 = (bf16[1152,768]{1,0:T(8,128)(2,1)}, bf16[1152,768]{1,0:T(8,128)(2,1)}, u32[]{:S(2)}, u32[]{:S(2)}) collective-permute-start(bf16[1152,768]{1,0:T(8,128)(2,1)} %slice.350), channel_id=1, source_target_pairs={{0,2},{2,0},{1,3},{3,1},{4,6},{6,4},{5,7},{7,5},{8,10},{10,8},{9,1... | collective-permute-start | bytes 5308424 | tf_op jit(solution)/shard_map/ppermute | solution.py:70
  109.0 11.8 %collective-permute-start.3 = (bf16[1152,512]{1,0:T(8,128)(2,1)S(1)}, bf16[1152,512]{1,0:T(8,128)(2,1)S(1)}, u32[]{:S(2)}, u32[]{:S(2)}) collective-permute-start(bf16[1152,512]{1,0:T(8,128)(2,1)S(1)} %slice.371), channel_id=1, source_target_pairs={{0,2},{2,0},{1,3},{3,1},{4,6},{6,4},{5,7},{7,5},{8,10},{10,8},{9,1... | collective-permute-start | bytes 3538952 | tf_op jit(solution)/shard_map/ppermute | solution.py:70
  125.7 11.4 %collective-permute-start.6 = (bf16[128,1152]{0,1:T(8,128)(2,1)S(1)}, bf16[128,1152]{0,1:T(8,128)(2,1)S(1)}, u32[]{:S(2)}, u32[]{:S(2)}) collective-permute-start(bf16[128,1152]{0,1:T(8,128)(2,1)S(1)} %get-tuple-element.40), channel_id=1, source_target_pairs={{0,16},{1,17},{16,0},{17,1},{2,18},{3,19},{18,2},{19,3},{4,20},{5,... | collective-permute-start | bytes 884744 | tf_op jit(solution)/shard_map/ppermute | solution.py:66
  128.7 13.4 %collective-permute-start.5 = (bf16[128,1152]{0,1:T(8,128)(2,1)S(1)}, bf16[128,1152]{0,1:T(8,128)(2,1)S(1)}, u32[]{:S(2)}, u32[]{:S(2)}) collective-permute-start(bf16[128,1152]{0,1:T(8,128)(2,1)S(1)} %get-tuple-element.40), channel_id=1, source_target_pairs={{0,17},{1,0},{16,1},{17,16},{2,19},{3,2},{18,3},{19,18},{4,21},{5,... | collective-permute-start | bytes 884744 | tf_op jit(solution)/shard_map/ppermute | solution.py:66
  129.8 12.3 %collective-permute-start.4 = (bf16[128,1152]{0,1:T(8,128)(2,1)S(1)}, bf16[128,1152]{0,1:T(8,128)(2,1)S(1)}, u32[]{:S(2)}, u32[]{:S(2)}) collective-permute-start(bf16[128,1152]{0,1:T(8,128)(2,1)S(1)} %get-tuple-element.40), channel_id=1, source_target_pairs={{0,1},{1,16},{16,17},{17,0},{2,3},{3,18},{18,19},{19,2},{4,5},{5,2... | collective-permute-start | bytes 884744 | tf_op jit(solution)/shard_map/ppermute | solution.py:66
  130.8 14.3 %collective-permute-start.7 = (bf16[128,1152]{0,1:T(8,128)(2,1)S(1)}, bf16[128,1152]{0,1:T(8,128)(2,1)S(1)}, u32[]{:S(2)}, u32[]{:S(2)}) collective-permute-start(bf16[128,1152]{0,1:T(8,128)(2,1)S(1)} %get-tuple-element.40), channel_id=1, source_target_pairs={{0,2},{2,0},{1,3},{3,1},{4,6},{6,4},{5,7},{7,5},{8,10},{10,8},{9,1... | collective-permute-start | bytes 884744 | tf_op jit(solution)/shard_map/ppermute | solution.py:70
  137.1 10.4 %collective-permute-start.10 = (bf16[128,1152]{0,1:T(8,128)(2,1)S(1)}, bf16[128,1152]{0,1:T(8,128)(2,1)S(1)}, u32[]{:S(2)}, u32[]{:S(2)}) collective-permute-start(bf16[128,1152]{0,1:T(8,128)(2,1)S(1)} %collective-permute-done.6), channel_id=1, source_target_pairs={{0,2},{2,0},{1,3},{3,1},{4,6},{6,4},{5,7},{7,5},{8,10},{10,8},{9,1... | collective-permute-start | bytes 884744 | tf_op jit(solution)/shard_map/ppermute | solution.py:70
  170.1 15.9 %collective-permute-start.12 = (bf16[128,1152]{0,1:T(8,128)(2,1)}, bf16[128,1152]{0,1:T(8,128)(2,1)S(1)}, u32[]{:S(2)}, u32[]{:S(2)}) collective-permute-start(bf16[128,1152]{0,1:T(8,128)(2,1)} %get-tuple-element.50), channel_id=1, source_target_pairs={{0,17},{1,0},{16,1},{17,16},{2,19},{3,2},{18,3},{19,18},{4,21},{5,... | collective-permute-start | bytes 884744 | tf_op jit(solution)/shard_map/ppermute | solution.py:66
  172.7 13.2 %collective-permute-start.14 = (bf16[128,1152]{0,1:T(8,128)(2,1)}, bf16[128,1152]{0,1:T(8,128)(2,1)S(1)}, u32[]{:S(2)}, u32[]{:S(2)}) collective-permute-start(bf16[128,1152]{0,1:T(8,128)(2,1)} %get-tuple-element.51), channel_id=1, source_target_pairs={{0,16},{1,17},{16,0},{17,1},{2,18},{3,19},{18,2},{19,3},{4,20},{5,... | collective-permute-start | bytes 884744 | tf_op jit(solution)/shard_map/ppermute | solution.py:66
  173.4 16.2 %collective-permute-start.13 = (bf16[128,1152]{0,1:T(8,128)(2,1)}, bf16[128,1152]{0,1:T(8,128)(2,1)}, u32[]{:S(2)}, u32[]{:S(2)}) collective-permute-start(bf16[128,1152]{0,1:T(8,128)(2,1)} %get-tuple-element.52), channel_id=1, source_target_pairs={{0,1},{1,16},{16,17},{17,0},{2,3},{3,18},{18,19},{19,2},{4,5},{5,2... | collective-permute-start | bytes 884744 | tf_op jit(solution)/shard_map/ppermute | solution.py:66
  194.2 11.7 %collective-permute-start.17 = (bf16[128,1152]{0,1:T(8,128)(2,1)S(1)}, bf16[128,1152]{0,1:T(8,128)(2,1)S(1)}, u32[]{:S(2)}, u32[]{:S(2)}) collective-permute-start(bf16[128,1152]{0,1:T(8,128)(2,1)S(1)} %get-tuple-element.34), channel_id=1, source_target_pairs={{0,16},{1,17},{16,0},{17,1},{2,18},{3,19},{18,2},{19,3},{4,20},{5,... | collective-permute-start | bytes 884744 | tf_op jit(solution)/shard_map/ppermute | solution.py:66
  195.1 13.0 %collective-permute-start.16 = (bf16[128,1152]{0,1:T(8,128)(2,1)S(1)}, bf16[128,1152]{0,1:T(8,128)(2,1)S(1)}, u32[]{:S(2)}, u32[]{:S(2)}) collective-permute-start(bf16[128,1152]{0,1:T(8,128)(2,1)S(1)} %get-tuple-element.34), channel_id=1, source_target_pairs={{0,17},{1,0},{16,1},{17,16},{2,19},{3,2},{18,3},{19,18},{4,21},{5,... | collective-permute-start | bytes 884744 | tf_op jit(solution)/shard_map/ppermute | solution.py:66
  196.4 14.9 %collective-permute-start.15 = (bf16[128,1152]{0,1:T(8,128)(2,1)S(1)}, bf16[128,1152]{0,1:T(8,128)(2,1)S(1)}, u32[]{:S(2)}, u32[]{:S(2)}) collective-permute-start(bf16[128,1152]{0,1:T(8,128)(2,1)S(1)} %get-tuple-element.34), channel_id=1, source_target_pairs={{0,1},{1,16},{16,17},{17,0},{2,3},{3,18},{18,19},{19,2},{4,5},{5,2... | collective-permute-start | bytes 884744 | tf_op jit(solution)/shard_map/ppermute | solution.py:66
  197.2 14.4 %collective-permute-start.18 = (bf16[128,1152]{0,1:T(8,128)(2,1)S(1)}, bf16[128,1152]{0,1:T(8,128)(2,1)S(1)}, u32[]{:S(2)}, u32[]{:S(2)}) collective-permute-start(bf16[128,1152]{0,1:T(8,128)(2,1)S(1)} %get-tuple-element.34), channel_id=1, source_target_pairs={{0,2},{2,0},{1,3},{3,1},{4,6},{6,4},{5,7},{7,5},{8,10},{10,8},{9,1... | collective-permute-start | bytes 884744 | tf_op jit(solution)/shard_map/ppermute | solution.py:70
  230.4 11.4 %collective-permute-start.25 = (bf16[128,1152]{0,1:T(8,128)(2,1)S(1)}, bf16[128,1152]{0,1:T(8,128)(2,1)S(1)}, u32[]{:S(2)}, u32[]{:S(2)}) collective-permute-start(bf16[128,1152]{0,1:T(8,128)(2,1)S(1)} %get-tuple-element.48), channel_id=1, source_target_pairs={{0,16},{1,17},{16,0},{17,1},{2,18},{3,19},{18,2},{19,3},{4,20},{5,... | collective-permute-start | bytes 884744 | tf_op jit(solution)/shard_map/ppermute | solution.py:66
  231.1 15.9 %collective-permute-start.24 = (bf16[128,1152]{0,1:T(8,128)(2,1)S(1)}, bf16[128,1152]{0,1:T(8,128)(2,1)S(1)}, u32[]{:S(2)}, u32[]{:S(2)}) collective-permute-start(bf16[128,1152]{0,1:T(8,128)(2,1)S(1)} %get-tuple-element.49), channel_id=1, source_target_pairs={{0,1},{1,16},{16,17},{17,0},{2,3},{3,18},{18,19},{19,2},{4,5},{5,2... | collective-permute-start | bytes 884744 | tf_op jit(solution)/shard_map/ppermute | solution.py:66
  265.6 146.0 %reduce-scatter.10.cloned.1.call-start = ((), (), s32[]{:S(2)}) async-start(), calls=%async_computation.9 | async-start | bytes 1880064
  271.3 226.2 %reduce-scatter.14.cloned.1.call-start = ((), (), s32[]{:S(2)}) async-start(), calls=%async_computation.11 | async-start | bytes 6580224
  347.0 71.0 %collective-permute-start.37 = (f32[18,256]{1,0:T(8,128)S(1)}, f32[18,256]{1,0:T(8,128)S(1)}, u32[]{:S(2)}, u32[]{:S(2)}) collective-permute-start(f32[18,256]{1,0:T(8,128)S(1)} %slice_select_fusion.2), channel_id=1, source_target_pairs={{0,2},{2,0},{1,3},{3,1},{4,6},{6,4},{5,7},{7,5},{8,10},{10,8},{9,1... | collective-permute-start | bytes 55304 | tf_op jit(solution)/shard_map/ppermute | solution.py:70
  413.6 10.6 %all-to-all-start.1 = ((bf16[4,36,512]{2,1,0:T(8,128)(2,1)}), bf16[4,36,512]{2,1,0:T(8,128)(2,1)S(1)}, u32[]{:S(2)}, u32[]{:S(2)}) async-start(bf16[4,36,512]{2,1,0:T(8,128)(2,1)} %bitcast.31), calls=%async_computation.1 | async-start | bytes 327680 | tf_op jit(solution)/shard_map/all_to_all | solution.py:339
  499.4 14.6 %all-to-all-start.3 = ((bf16[4,18,2688]{2,1,0:T(8,128)(2,1)}), bf16[4,18,2688]{2,1,0:T(8,128)(2,1)S(1)}, u32[]{:S(2)}, u32[]{:S(2)}) async-start(bf16[4,18,2688]{2,1,0:T(8,128)(2,1)} %reshape.438), calls=%async_computation.3 | async-start | bytes 1032192 | tf_op jit(solution)/shard_map/all_to_all | solution.py:285
  (122 other events, 1311.2 us)
Sparse Core Ops, SparseCore 0:
  24.9 48.3 all-gather.7
  75.5 59.9 all-gather.9
  265.7 69.5 reduce-scatter.11
  338.4 73.1 reduce-scatter.9
  414.9 82.5 reduce-scatter.13
